TPU v7x, 32 devices: a whole 2x2x4 slice. The times are simulated.
32 devices in a mesh: area: 4 (over y, core), pos: 8 (over z, x).
Axes of the slice: x: 2, y: 2, z: 4, core: 2. Of those that a mesh axis runs over, the one named last changes fastest.
Arguments:
- exit_wave: bfloat16 [128, 2, 128, 128], P(('area', 'pos')), may hold values from -6 to 6
- amplitude: bfloat16 [128, 128, 128], P(('area', 'pos')), may hold values from 0.19921875 to 5
- probe: float32 [2, 128, 128], replicated, may hold values from -4 to 4
- offsets: int32 [128, 2], P(('area', 'pos')), may hold values from 0 to 127
- owner: int32 [128, 1], P(('area', 'pos')), may hold values from 0 to 7; in each aligned block of 4 rows (0 to 3, 4 to 7, ...) at most 2 rows name the same one
Outputs:
- new_wave: bfloat16 [128, 2, 128, 128], P(('area', 'pos'))
- object_field: float32 [2, 512, 1024], P(None, 'area', 'pos')
Inputs may be any that keep to these rules, and one draw needn't show every extreme that they name: owner names the object tile column that holds the position's patch centre; of the 4 positions of one device at most 2 name the same tile.
All inputs are finite; a program needn't handle non-finite values.
Results may differ from a plain program's by a relative error of at most 0.0059.
Values may be sent and summed in bfloat16 or wider, within the bound.
No kernel may reach another device: no remote copies, remote signals or barrier semaphores. Data moves between devices by JAX's collectives and lax.ppermute only.
A program may use at most 64 MiB of HBM per device.

v0:
```python
import math
import jax
import jax.numpy as jnp
from jax import lax
from jax.sharding import PartitionSpec as P

F = 128
TS = 128
C = 2


def passed_along(value, axis, steps):
    count = lax.axis_size(axis)
    first, last = (max(0, -steps), min(count, count - steps))
    return lax.ppermute(value, axis, [(source, source + steps) for source in range(first, last)])


def extended(cells, sides, width):
    for axis, dim in sides:
        count = lax.axis_size(axis)
        ends = count - 1
        head = lax.slice_in_dim(cells, 0, width, axis=dim)
        tail = lax.slice_in_dim(cells, cells.shape[dim] - width, cells.shape[dim], axis=dim)
        cells = jnp.concatenate(
            [
                lax.ppermute(tail, axis, [(i, (i + 1) % count) for i in range(ends)]),
                cells,
                lax.ppermute(head, axis, [((i + 1) % count, i) for i in range(ends)]),
            ],
            axis=dim,
        )
    return cells


def fold_rows(canvas):
    margin = F // 2
    summed = canvas
    for step in (1, -1):
        edge = canvas[:, TS + margin :, :] if step == 1 else canvas[:, :margin, :]
        arrived = passed_along(edge, "area", step)
        first = margin if step == 1 else TS
        summed = summed.at[:, first : first + margin, :].add(arrived)
    return summed[:, margin : margin + TS, :]


def fold_columns(canvas):
    margin = F // 2
    summed = canvas
    for step in (1, -1):
        edge = canvas[:, :, TS + margin :] if step == 1 else canvas[:, :, :margin]
        arrived = passed_along(edge, "pos", step)
        first = margin if step == 1 else TS
        summed = summed.at[:, :, first : first + margin].add(arrived)
    return summed[:, :, margin : margin + TS]


def left_multiply(mat_re, mat_im, data_re, data_im):
    highest = lax.Precision.HIGHEST
    out_re = jnp.einsum("kn,bnm->bkm", mat_re, data_re, precision=highest) - jnp.einsum(
        "kn,bnm->bkm", mat_im, data_im, precision=highest
    )
    out_im = jnp.einsum("kn,bnm->bkm", mat_re, data_im, precision=highest) + jnp.einsum(
        "kn,bnm->bkm", mat_im, data_re, precision=highest
    )
    return (out_re, out_im)


def right_multiply(data_re, data_im, mat_re, mat_im):
    highest = lax.Precision.HIGHEST
    out_re = jnp.einsum("bkm,ml->bkl", data_re, mat_re, precision=highest) - jnp.einsum(
        "bkm,ml->bkl", data_im, mat_im, precision=highest
    )
    out_im = jnp.einsum("bkm,ml->bkl", data_re, mat_im, precision=highest) + jnp.einsum(
        "bkm,ml->bkl", data_im, mat_re, precision=highest
    )
    return (out_re, out_im)


def cut_patches(source, row_starts, col_starts):
    return jax.vmap(lambda r, c: lax.dynamic_slice(source, (jnp.int32(0), r, c), (2, F, F)))(
        row_starts, col_starts
    )


def weighted_waves(waves_bf, probe_re, probe_im):
    waves_f = waves_bf.astype(jnp.float32)
    first = probe_re * waves_f[:, 0] + probe_im * waves_f[:, 1]
    second = probe_re * waves_f[:, 1] - probe_im * waves_f[:, 0]
    return jnp.stack([first, second], 1).astype(jnp.bfloat16)


def accumulate(contrib, meta, power_map):
    live = meta[:, 2]
    ordering = jnp.argsort(1 - live, stable=True)
    live_count = jnp.sum(live)

    def add_one(number, canvas):
        chosen = ordering[number]
        piece = jnp.concatenate([contrib[chosen].astype(jnp.float32), power_map[None]], 0)
        where = (jnp.int32(0), meta[chosen, 0], meta[chosen, 1])
        old = lax.dynamic_slice(canvas, where, (3, F, F))
        return lax.dynamic_update_slice(canvas, old + piece, where)

    canvas = lax.fori_loop(0, live_count, add_one, jnp.zeros((3, TS + F, TS + F), jnp.float32))
    summed = fold_columns(fold_rows(canvas))
    return (summed[0:2] / (summed[2] + 0.1)[None], ordering, live_count)


def relaxed_update(waves_bf, amps_bf, patch_bf, probe_re, probe_im):
    pixel = jnp.arange(F, dtype=jnp.int32)
    product = pixel[:, None] * pixel[None, :] % F
    angle = product.astype(jnp.float32) * (2.0 * math.pi / F)
    scale_by = 1.0 / math.sqrt(F)
    twiddle_re = jnp.cos(angle) * scale_by
    twiddle_im = -jnp.sin(angle) * scale_by
    waves_f = waves_bf.astype(jnp.float32)
    patch_f = patch_bf.astype(jnp.float32)
    proj_re = probe_re * patch_f[:, 0] - probe_im * patch_f[:, 1]
    proj_im = probe_re * patch_f[:, 1] + probe_im * patch_f[:, 0]
    trial_re = 2.0 * proj_re - waves_f[:, 0]
    trial_im = 2.0 * proj_im - waves_f[:, 1]
    half_re, half_im = left_multiply(twiddle_re, twiddle_im, trial_re, trial_im)
    spectrum_re, spectrum_im = right_multiply(half_re, half_im, twiddle_re, twiddle_im)
    modulus = jnp.sqrt(spectrum_re * spectrum_re + spectrum_im * spectrum_im + 0.01)
    ratio = amps_bf.astype(jnp.float32) / modulus
    fitted_re = spectrum_re * ratio
    fitted_im = spectrum_im * ratio
    half_re, half_im = left_multiply(twiddle_re, -twiddle_im, fitted_re, fitted_im)
    back_re, back_im = right_multiply(half_re, half_im, twiddle_re, -twiddle_im)
    new_re = 0.75 * waves_f[:, 0] - 0.5 * proj_re + 0.75 * back_re
    new_im = 0.75 * waves_f[:, 1] - 0.5 * proj_im + 0.75 * back_im
    return jnp.stack([new_re, new_im], 1).astype(jnp.bfloat16)


def body(exit_wave, amplitude, probe, offsets, owner):
    margin = F // 2
    columns_count = lax.axis_size("pos")
    probe_re = probe[0]
    probe_im = probe[1]
    power_map = probe_re * probe_re + probe_im * probe_im
    target = owner[:, 0]
    one_hot = (target[:, None] == jnp.arange(columns_count, dtype=jnp.int32)[None, :]).astype(
        jnp.int32
    )
    rank_in = jnp.sum((jnp.cumsum(one_hot, axis=0) - 1) * one_hot, axis=1)
    slot_flat = target * C + rank_in
    slot_total = columns_count * C
    described = jnp.concatenate([offsets, jnp.ones((offsets.shape[0], 1), jnp.int32)], 1)
    send_meta = jnp.zeros((slot_total, 3), jnp.int32).at[slot_flat].set(described)
    contrib = weighted_waves(exit_wave, probe_re, probe_im)
    send_wave = jnp.zeros((slot_total, 2, F, F), jnp.bfloat16).at[slot_flat].set(contrib)
    got_wave, got_meta = (
        lax.all_to_all(send_wave, "pos", split_axis=0, concat_axis=0, tiled=True),
        lax.all_to_all(send_meta, "pos", split_axis=0, concat_axis=0, tiled=True),
    )
    object_tile, ordering, live_count = accumulate(got_wave, got_meta, power_map)
    object_half = object_tile.astype(jnp.bfloat16)
    strip = extended(object_half, (("area", 1),), margin)
    band_rows = lax.all_gather(strip, "pos", axis=2, tiled=True)
    band_rows = jnp.pad(band_rows, ((0, 0), (0, 0), (margin, margin)))
    own_patch = cut_patches(band_rows, offsets[:, 0], target * TS + offsets[:, 1])
    new_wave = relaxed_update(exit_wave, amplitude, own_patch, probe_re, probe_im)
    return (new_wave, object_tile)


def solution(mesh):
    return jax.shard_map(
        body,
        mesh=mesh,
        in_specs=(
            P(("area", "pos"), None, None, None),
            P(("area", "pos"), None, None),
            P(),
            P(("area", "pos"), None),
            P(("area", "pos"), None),
        ),
        out_specs=(P(("area", "pos"), None, None, None), P(None, "area", "pos")),
        check_vma=False,
    )
```

profile of v0, /device:TPU:0, one launch (start us, length us, event | category | flops | bytes accessed | tf_op | source)
XLA Modules:
  0.0 265.7 jit_solution(17552448648142886674)
XLA Ops:
  7.2 0.7 fusion.55
  7.9 0.8 select_reduce_fusion
  8.8 0.8 copy.121
  9.5 0.8 compare_select_fusion.1
  10.3 1.2 scatter_custom_fusion
  11.5 7.3 %all-to-all-start = ((s32[8,2,3]{2,1,0:T(2,128)}), s32[8,2,3]{2,1,0:T(2,128)S(1)}, u32[]{:S(2)}, u32[]{:S(2)}) async-start(s32[8,2,3]{2,1,0:T(2,128)} %bitcast.10), calls=%async_computation | async-start | bytes 16384 | tf_op jit(solution)/shard_map/all_to_all | solution.py:154
  18.7 1.0 copy_convert_fusion
  19.7 0.9 slice_bitcast_fusion.3
  20.8 1.2 broadcast_in_dim.11
  22.0 2.2 scatter_fusion
  24.2 1.1 all-to-all-done
  25.3 5.0 %all-to-all-start.1 = ((bf16[16,2,128,128]{3,2,1,0:T(8,128)(2,1)}), bf16[16,2,128,128]{3,2,1,0:T(8,128)(2,1)S(1)}, u32[]{:S(2)}, u32[]{:S(2)}) async-start(bf16[16,2,128,128]{3,2,1,0:T(8,128)(2,1)} %scatter_fusion), calls=%async_computation.1 | async-start | bytes 2097152 | tf_op jit(solution)/shard_map/all_to_all | solution.py:153
  31.1 1.3 sort.17
  32.3 23.4 %all-to-all-done.1 = bf16[16,2,128,128]{3,2,1,0:T(8,128)(2,1)S(1)} async-done(((bf16[16,2,128,128]{3,2,1,0:T(8,128)(2,1)}), bf16[16,2,128,128]{3,2,1,0:T(8,128)(2,1)S(1)}, u32[]{:S(2)}, u32[]{:S(2)}) %all-to-all-start.1) | async-done | bytes 1048608 | tf_op jit(solution)/shard_map/all_to_all | solution.py:153
  55.8 62.8 %while.15 = (s32[]{:T(128)}, f32[3,256,256]{2,1,0:T(8,128)S(1)}, s32[]{:T(128)}, s32[16]{0:T(128)S(1)}, s32[16,3]{0,1:T(4,128)S(1)}, /*index=5*/bf16[16,2,128,12...) while((s32[]{:T(128)}, f32[3,256,256]{2,1,0:T(8,128)S(1)}, ...), condition=%wide.region_7.8_spmd, body=%wide.region_6.7_spmd.sunk | while | flops 131086 | bytes 1179941 | solution.py:104
  58.7 0.7 constant_dynamic-slice_fusion.5
  63.3 2.8 %dynamic_update_slice.4 = f32[3,256,256]{2,1,0:T(8,128)S(1)} dynamic-update-slice(f32[3,256,256]{2,1,0:T(8,128)S(1)} %get-tuple-element.257, f32[3,128,128]{2,1,0:T(8,128)S(1)} %maximum_add_fusion.2, s32[]{:T(128)} %constant.154.clone.1..sunk, s32[]{:T(128)S(6)} %select_n.138, s32[]{:T(128)S(6)} %select_n.139) | dynamic-update-slice | bytes 393220 | tf_op jit(solution)/shard_map/while/body/dynamic_update_slice | solution.py:102
  69.0 0.7 constant_dynamic-slice_fusion.5
  73.5 2.9 %dynamic_update_slice.4 = f32[3,256,256]{2,1,0:T(8,128)S(1)} dynamic-update-slice(f32[3,256,256]{2,1,0:T(8,128)S(1)} %get-tuple-element.257, f32[3,128,128]{2,1,0:T(8,128)S(1)} %maximum_add_fusion.2, s32[]{:T(128)} %constant.154.clone.1..sunk, s32[]{:T(128)S(6)} %select_n.138, s32[]{:T(128)S(6)} %select_n.139) | dynamic-update-slice | bytes 393220 | tf_op jit(solution)/shard_map/while/body/dynamic_update_slice | solution.py:102
  79.3 0.7 constant_dynamic-slice_fusion.5
  83.9 2.9 %dynamic_update_slice.4 = f32[3,256,256]{2,1,0:T(8,128)S(1)} dynamic-update-slice(f32[3,256,256]{2,1,0:T(8,128)S(1)} %get-tuple-element.257, f32[3,128,128]{2,1,0:T(8,128)S(1)} %maximum_add_fusion.2, s32[]{:T(128)} %constant.154.clone.1..sunk, s32[]{:T(128)S(6)} %select_n.138, s32[]{:T(128)S(6)} %select_n.139) | dynamic-update-slice | bytes 393220 | tf_op jit(solution)/shard_map/while/body/dynamic_update_slice | solution.py:102
  89.7 0.7 constant_dynamic-slice_fusion.5
  94.3 2.8 %dynamic_update_slice.4 = f32[3,256,256]{2,1,0:T(8,128)S(1)} dynamic-update-slice(f32[3,256,256]{2,1,0:T(8,128)S(1)} %get-tuple-element.257, f32[3,128,128]{2,1,0:T(8,128)S(1)} %maximum_add_fusion.2, s32[]{:T(128)} %constant.154.clone.1..sunk, s32[]{:T(128)S(6)} %select_n.138, s32[]{:T(128)S(6)} %select_n.139) | dynamic-update-slice | bytes 393220 | tf_op jit(solution)/shard_map/while/body/dynamic_update_slice | solution.py:102
  100.0 0.7 constant_dynamic-slice_fusion.5
  104.5 3.0 %dynamic_update_slice.4 = f32[3,256,256]{2,1,0:T(8,128)S(1)} dynamic-update-slice(f32[3,256,256]{2,1,0:T(8,128)S(1)} %get-tuple-element.257, f32[3,128,128]{2,1,0:T(8,128)S(1)} %maximum_add_fusion.2, s32[]{:T(128)} %constant.154.clone.1..sunk, s32[]{:T(128)S(6)} %select_n.138, s32[]{:T(128)S(6)} %select_n.139) | dynamic-update-slice | bytes 393220 | tf_op jit(solution)/shard_map/while/body/dynamic_update_slice | solution.py:102
  115.0 2.9 %dynamic_update_slice.4 = f32[3,256,256]{2,1,0:T(8,128)S(1)} dynamic-update-slice(f32[3,256,256]{2,1,0:T(8,128)S(1)} %get-tuple-element.257, f32[3,128,128]{2,1,0:T(8,128)S(1)} %maximum_add_fusion.2, s32[]{:T(128)} %constant.154.clone.1..sunk, s32[]{:T(128)S(6)} %select_n.138, s32[]{:T(128)S(6)} %select_n.139) | dynamic-update-slice | bytes 393220 | tf_op jit(solution)/shard_map/while/body/dynamic_update_slice | solution.py:102
  118.6 1.3 collective-permute-start
  119.9 1.0 collective-permute-done
  121.0 1.3 collective-permute-start.1
  122.3 2.0 collective-permute-done.1
  124.5 1.3 collective-permute-start.2
  125.9 1.3 collective-permute-start.3
  127.2 1.8 collective-permute-done.2
  129.1 1.3 scatter-add.16
  130.5 54.6 %collective-permute-done.3 = f32[3,128,64]{2,1,0:T(8,128)S(1)} collective-permute-done((f32[3,128,64]{2,1,0:T(8,128)S(1)}, f32[3,128,64]{2,1,0:T(8,128)S(1)}, u32[]{:S(2)}, u32[]{:S(2)}) %collective-permute-start.3) | collective-permute-done | bytes 98336 | tf_op jit(solution)/shard_map/ppermute | solution.py:15
  185.6 0.8 fusion.145
  186.4 4.8 %collective-permute-start.4 = (bf16[2,64,128]{2,1,0:T(8,128)(2,1)S(1)}, bf16[2,64,128]{2,1,0:T(8,128)(2,1)S(1)}, u32[]{:S(2)}, u32[]{:S(2)}) collective-permute-start(bf16[2,64,128]{2,1,0:T(8,128)(2,1)S(1)} %get-tuple-element.161), channel_id=1, source_target_pairs={{0,8},{8,16},{16,24},{1,9},{9,17},{17,25},{2,10},{10,18},{18,26},{... | collective-permute-start | bytes 98312 | tf_op jit(solution)/shard_map/ppermute | solution.py:26
  191.2 1.3 collective-permute-start.5
  192.5 2.3 collective-permute-done.5
  194.8 0.7 pad_maximum_fusion.2
  195.6 40.4 %all-gather.2.cloned.1.call-done = bf16[2,256,1024]{2,1,0:T(8,128)(2,1)} async-done(((bf16[2,256,128]{2,1,0:T(8,128)(2,1)}), bf16[2,256,1024]{2,1,0:T(8,128)(2,1)}) %all-gather.2.cloned.1.call-update) | async-done | bytes 1048592 | tf_op jit(solution)/shard_map/all_gather | solution.py:159
  236.0 1.9 pad.13
  237.9 8.0 %while.16 = (s32[]{:T(128)}, bf16[2,256,1152]{2,1,0:T(8,128)(2,1)S(1)}, s32[4,3]{1,0:T(4,128)S(1)}, bf16[4,2,128,128]{3,2,0,1:T(8,128)(2,1)S(1)}, s32[]{:T(128)}) while((s32[]{:T(128)}, bf16[2,256,1152]{2,1,0:T(8,128)(2,1)S(1)}, s32[4,3]{1,0:T(4,128)S(1)}, bf16[4,2,128,128]{3,2,0,1:T(8,128)(2,1)S(1)}, s32[]{:T(128)}) %tuple.76), condition=%wide.while_cond.4, body=%wide.while_body.4.sunk | while | flops 2 | bytes 131189 | solution.py:80
  238.5 1.3 bitcast_dynamic-update-slice_fusion.2
  240.5 1.3 bitcast_dynamic-update-slice_fusion.2
  242.4 1.3 bitcast_dynamic-update-slice_fusion.2
  244.3 1.3 bitcast_dynamic-update-slice_fusion.2
  246.0 0.7 fusion.18
  246.8 0.8 fusion.17
  247.5 0.8 fusion.7
  248.3 0.7 fusion.28
  249.0 0.7 fusion.42
  249.7 0.7 fusion.6
  250.5 0.7 convolution_add_fusion.2
  251.2 0.7 convolution_subtract_fusion.2
  252.0 0.8 fusion.34
  252.8 0.8 fusion.38
  253.6 0.8 fusion.5
  254.4 0.7 fusion.36
  255.1 0.7 fusion.23
  255.8 0.8 fusion.4
  256.6 0.7 fusion.11
  257.4 0.7 fusion.10
  258.1 0.7 copy.99
  (60 shorter events, 9.6 us)
Async XLA Ops:
  11.5 13.8 %all-to-all-start = ((s32[8,2,3]{2,1,0:T(2,128)}), s32[8,2,3]{2,1,0:T(2,128)S(1)}, u32[]{:S(2)}, u32[]{:S(2)}) async-start(s32[8,2,3]{2,1,0:T(2,128)} %bitcast.10), calls=%async_computation | async-start | bytes 16384 | tf_op jit(solution)/shard_map/all_to_all | solution.py:154
  24.2 6.2 %copy-start.1 = (f32[2,128,128]{2,1,0:T(8,128)S(1)}, f32[2,128,128]{2,1,0:T(8,128)}, u32[]{:S(2)}) copy-start(f32[2,128,128]{2,1,0:T(8,128)} %param.17) | copy-start | bytes 393220
  25.3 30.5 %all-to-all-start.1 = ((bf16[16,2,128,128]{3,2,1,0:T(8,128)(2,1)}), bf16[16,2,128,128]{3,2,1,0:T(8,128)(2,1)S(1)}, u32[]{:S(2)}, u32[]{:S(2)}) async-start(bf16[16,2,128,128]{3,2,1,0:T(8,128)(2,1)} %scatter_fusion), calls=%async_computation.1 | async-start | bytes 2097152 | tf_op jit(solution)/shard_map/all_to_all | solution.py:153
  30.3 205.7 %all-gather.2.cloned.1.call-start = ((), (), s32[]{:S(2)}) async-start(), calls=%async_computation.2 | async-start | bytes 1179648 | tf_op jit(solution)/shard_map/all_gather | solution.py:159
  118.6 2.4 collective-permute-start
  121.0 3.3 %collective-permute-start.1 = (f32[3,64,256]{2,1,0:T(8,128)S(1)}, f32[3,64,256]{2,1,0:T(8,128)S(1)}, u32[]{:S(2)}, u32[]{:S(2)}) collective-permute-start(f32[3,64,256]{2,1,0:T(8,128)S(1)} %get-tuple-element.153), channel_id=1, source_target_pairs={{8,0},{16,8},{24,16},{9,1},{17,9},{25,17},{10,2},{18,10},{26,18},{... | collective-permute-start | bytes 589832 | tf_op jit(solution)/shard_map/ppermute | solution.py:15
  124.5 4.5 %collective-permute-start.2 = (f32[3,128,64]{2,1,0:T(8,128)S(1)}, f32[3,128,64]{2,1,0:T(8,128)S(1)}, u32[]{:S(2)}, u32[]{:S(2)}) collective-permute-start(f32[3,128,64]{2,1,0:T(8,128)S(1)} %get-tuple-element.152), channel_id=1, source_target_pairs={{0,1},{1,2},{2,3},{3,4},{4,5},{5,6},{6,7},{8,9},{9,10},{10,11},{11... | collective-permute-start | bytes 294920 | tf_op jit(solution)/shard_map/ppermute | solution.py:15
  125.9 59.2 %collective-permute-start.3 = (f32[3,128,64]{2,1,0:T(8,128)S(1)}, f32[3,128,64]{2,1,0:T(8,128)S(1)}, u32[]{:S(2)}, u32[]{:S(2)}) collective-permute-start(f32[3,128,64]{2,1,0:T(8,128)S(1)} %get-tuple-element.151), channel_id=1, source_target_pairs={{1,0},{2,1},{3,2},{4,3},{5,4},{6,5},{7,6},{9,8},{10,9},{11,10},{12... | collective-permute-start | bytes 294920 | tf_op jit(solution)/shard_map/ppermute | solution.py:15
  186.4 6.1 %collective-permute-start.4 = (bf16[2,64,128]{2,1,0:T(8,128)(2,1)S(1)}, bf16[2,64,128]{2,1,0:T(8,128)(2,1)S(1)}, u32[]{:S(2)}, u32[]{:S(2)}) collective-permute-start(bf16[2,64,128]{2,1,0:T(8,128)(2,1)S(1)} %get-tuple-element.161), channel_id=1, source_target_pairs={{0,8},{8,16},{16,24},{1,9},{9,17},{17,25},{2,10},{10,18},{18,26},{... | collective-permute-start | bytes 98312 | tf_op jit(solution)/shard_map/ppermute | solution.py:26
  191.2 3.6 %collective-permute-start.5 = (bf16[2,64,128]{2,1,0:T(8,128)(2,1)S(1)}, bf16[2,64,128]{2,1,0:T(8,128)(2,1)S(1)}, u32[]{:S(2)}, u32[]{:S(2)}) collective-permute-start(bf16[2,64,128]{2,1,0:T(8,128)(2,1)S(1)} %get-tuple-element.162), channel_id=1, source_target_pairs={{8,0},{16,8},{24,16},{9,1},{17,9},{25,17},{10,2},{18,10},{26,18},{... | collective-permute-start | bytes 98312 | tf_op jit(solution)/shard_map/ppermute | solution.py:28
  249.7 2.2 copy-start
Sparse Core Ops, SparseCore 0:
  195.6 40.3 all-gather.1
where the time goes:
time: 267 us; the launch traced here: 266 us
  waiting for transfers between devices  127 us (48%)
  local copies, waits for them, and re-layouts  43.4 us (16%)
  loops' own time  37.5 us (14%)
  starting transfers between devices  23.6 us (9%)
  between operations  14.4 us (5%)
  matrix products  12 us (4%)
  other arithmetic  8.18 us (3%)
    ppermute x4, waiting for transfers between devices, passed_along(): lax.ppermute(value, axis, [(source, source + steps) for source in range(f...  59.5 us
    all_gather x1, waiting for transfers between devices, body(): band_rows = lax.all_gather(strip, 'pos', axis=2, tiled=True)  40.4 us
    another operation x1, loops' own time, accumulate(): lax.fori_loop(0, live_count, add_one, jnp.zeros((3, TS + F, TS + F), jnp....  37.2 us
    all_to_all x1, waiting for transfers between devices, body(): lax.all_to_all(send_wave, 'pos', split_axis=0, concat_axis=0, tiled=True)  23.4 us
    dynamic_update_slice x6, local copies, waits for them, and re-layouts, add_one(): return lax.dynamic_update_slice(canvas, old + piece, where)  17.2 us
    gather x12, local copies, waits for them, and re-layouts  7.71 us
    all_to_all x1, starting transfers between devices, body(): lax.all_to_all(send_meta, 'pos', split_axis=0, concat_axis=0, tiled=True)  7.28 us
  transfers between devices with their start and end apart: 9, of which 8 were waited for; matrix products, arithmetic and copies ran while one was open for 3% of the time, Pallas kernels for 0%

commit v1 on v0

--- a/solution.py
+++ b/solution.py
@@ -7,6 +7,14 @@
 F = 128
 TS = 128
 C = 2
+
+
+def gather_from_all(array, axis, dim):
+    peers = lax.axis_size(axis)
+    repeats = [peers if d == dim else 1 for d in range(array.ndim)]
+    return lax.all_to_all(
+        jnp.tile(array, repeats), axis, split_axis=dim, concat_axis=dim, tiled=True
+    )
 
 
 def passed_along(value, axis, steps):
@@ -156,7 +164,7 @@
     object_tile, ordering, live_count = accumulate(got_wave, got_meta, power_map)
     object_half = object_tile.astype(jnp.bfloat16)
     strip = extended(object_half, (("area", 1),), margin)
-    band_rows = lax.all_gather(strip, "pos", axis=2, tiled=True)
+    band_rows = gather_from_all(strip, "pos", 2)
     band_rows = jnp.pad(band_rows, ((0, 0), (0, 0), (margin, margin)))
     own_patch = cut_patches(band_rows, offsets[:, 0], target * TS + offsets[:, 1])
     new_wave = relaxed_update(exit_wave, amplitude, own_patch, probe_re, probe_im)

time: 267 us -> 252 us (0.944)
  between operations: 14.4 us -> 1 us
  waiting for transfers between devices: 127 us -> 115 us
  starting transfers between devices: 23.6 us -> 27.8 us
  local copies, waits for them, and re-layouts: 43.4 us -> 46.4 us
    all_gather x1 -> x0, waiting for transfers between devices: 40.4 us -> none  [body(): band_rows = lax.all_gather(strip, 'pos', axis=2, tiled=True)]
    all_to_all x0 -> x1, waiting for transfers between devices: none -> 26.4 us  [gather_from_all(): lax.all_to_all(jnp.tile(array, repeats), axis, split_axis=dim, concat_axi...]
    all_to_all x0 -> x1, starting transfers between devices: none -> 4.19 us  [gather_from_all(): lax.all_to_all(jnp.tile(array, repeats), axis, split_axis=dim, concat_axi...]
    gather x12 -> x20, local copies, waits for them, and re-layouts: 7.71 us -> 8.8 us
  transfers between devices with their start and end apart: 9 -> 9, of which waited for: 8 -> 8; matrix products, arithmetic and copies ran while one was open for 3% -> 4% of each run, Pallas kernels for 0% -> 0%
where the time goes in v1:
time: 252 us; the launch traced here: 250 us
  waiting for transfers between devices  115 us (46%)
  local copies, waits for them, and re-layouts  46.4 us (18%)
  loops' own time  40 us (16%)
  starting transfers between devices  27.8 us (11%)
  matrix products  12 us (5%)
  other arithmetic  7.59 us (3%)
    ppermute x4, waiting for transfers between devices, passed_along(): lax.ppermute(value, axis, [(source, source + steps) for source in range(f...  62 us
    another operation x1, loops' own time, accumulate(): lax.fori_loop(0, live_count, add_one, jnp.zeros((3, TS + F, TS + F), jnp....  39.7 us
    all_to_all x1, waiting for transfers between devices, gather_from_all(): lax.all_to_all(jnp.tile(array, repeats), axis, split_axis=dim, concat_axi...  26.4 us
    all_to_all x1, waiting for transfers between devices, body(): lax.all_to_all(send_wave, 'pos', split_axis=0, concat_axis=0, tiled=True)  23.3 us
    dynamic_update_slice x6, local copies, waits for them, and re-layouts, add_one(): return lax.dynamic_update_slice(canvas, old + piece, where)  17.2 us
    gather x20, local copies, waits for them, and re-layouts  8.8 us
    all_to_all x1, starting transfers between devices, body(): lax.all_to_all(send_meta, 'pos', split_axis=0, concat_axis=0, tiled=True)  7.28 us
    ppermute x4, starting transfers between devices, passed_along(): lax.ppermute(value, axis, [(source, source + steps) for source in range(f...  5.19 us
  transfers between devices with their start and end apart: 9, of which 8 were waited for; matrix products, arithmetic and copies ran while one was open for 4% of the time, Pallas kernels for 0%

profile of v1, /device:TPU:0, one launch (start us, length us, event | category | flops | bytes accessed | tf_op | source)
XLA Modules:
  0.0 249.8 jit_solution(2084400669919838624)
XLA Ops:
  0.6 0.7 fusion.55
  1.4 0.8 select_reduce_fusion
  2.2 0.8 copy.126
  3.0 0.8 compare_select_fusion.1
  3.8 1.2 scatter_custom_fusion
  4.9 7.3 %all-to-all-start = ((s32[8,2,3]{2,1,0:T(2,128)}), s32[8,2,3]{2,1,0:T(2,128)S(1)}, u32[]{:S(2)}, u32[]{:S(2)}) async-start(s32[8,2,3]{2,1,0:T(2,128)} %bitcast.10), calls=%async_computation | async-start | bytes 16384 | tf_op jit(solution)/shard_map/all_to_all | solution.py:162
  12.2 1.0 copy_convert_fusion
  13.2 0.9 slice_bitcast_fusion.3
  14.2 1.2 broadcast_in_dim.11
  15.4 2.2 scatter_fusion
  17.7 1.1 all-to-all-done
  18.7 5.0 %all-to-all-start.1 = ((bf16[16,2,128,128]{3,2,1,0:T(8,128)(2,1)}), bf16[16,2,128,128]{3,2,1,0:T(8,128)(2,1)S(1)}, u32[]{:S(2)}, u32[]{:S(2)}) async-start(bf16[16,2,128,128]{3,2,1,0:T(8,128)(2,1)} %scatter_fusion), calls=%async_computation.1 | async-start | bytes 2097152 | tf_op jit(solution)/shard_map/all_to_all | solution.py:161
  24.5 1.3 sort.17
  25.8 23.3 %all-to-all-done.1 = bf16[16,2,128,128]{3,2,1,0:T(8,128)(2,1)S(1)} async-done(((bf16[16,2,128,128]{3,2,1,0:T(8,128)(2,1)}), bf16[16,2,128,128]{3,2,1,0:T(8,128)(2,1)S(1)}, u32[]{:S(2)}, u32[]{:S(2)}) %all-to-all-start.1) | async-done | bytes 1048608 | tf_op jit(solution)/shard_map/all_to_all | solution.py:161
  49.3 65.8 %while.15 = (s32[]{:T(128)}, f32[3,256,256]{2,1,0:T(8,128)S(1)}, s32[]{:T(128)}, s32[16]{0:T(128)S(1)}, s32[16,3]{0,1:T(4,128)S(1)}, /*index=5*/bf16[16,2,128,12...) while((s32[]{:T(128)}, f32[3,256,256]{2,1,0:T(8,128)S(1)}, ...), condition=%wide.region_7.8_spmd, body=%wide.region_6.7_spmd.sunk | while | flops 131086 | bytes 1179941 | solution.py:112
  49.9 0.7 dynamic_slice.26
  52.7 0.7 constant_dynamic-slice_fusion.7
  57.2 2.8 %dynamic_update_slice.4 = f32[3,256,256]{2,1,0:T(8,128)S(1)} dynamic-update-slice(f32[3,256,256]{2,1,0:T(8,128)S(1)} %get-tuple-element.257, f32[3,128,128]{2,1,0:T(8,128)S(1)} %maximum_add_fusion.2, s32[]{:T(128)} %constant.154.clone.1..sunk, s32[]{:T(128)S(6)} %select_n.138, s32[]{:T(128)S(6)} %select_n.139) | dynamic-update-slice | bytes 393220 | tf_op jit(solution)/shard_map/while/body/dynamic_update_slice | solution.py:110
  60.7 0.7 dynamic_slice.26
  63.4 0.7 constant_dynamic-slice_fusion.7
  68.0 2.9 %dynamic_update_slice.4 = f32[3,256,256]{2,1,0:T(8,128)S(1)} dynamic-update-slice(f32[3,256,256]{2,1,0:T(8,128)S(1)} %get-tuple-element.257, f32[3,128,128]{2,1,0:T(8,128)S(1)} %maximum_add_fusion.2, s32[]{:T(128)} %constant.154.clone.1..sunk, s32[]{:T(128)S(6)} %select_n.138, s32[]{:T(128)S(6)} %select_n.139) | dynamic-update-slice | bytes 393220 | tf_op jit(solution)/shard_map/while/body/dynamic_update_slice | solution.py:110
  78.9 2.9 %dynamic_update_slice.4 = f32[3,256,256]{2,1,0:T(8,128)S(1)} dynamic-update-slice(f32[3,256,256]{2,1,0:T(8,128)S(1)} %get-tuple-element.257, f32[3,128,128]{2,1,0:T(8,128)S(1)} %maximum_add_fusion.2, s32[]{:T(128)} %constant.154.clone.1..sunk, s32[]{:T(128)S(6)} %select_n.138, s32[]{:T(128)S(6)} %select_n.139) | dynamic-update-slice | bytes 393220 | tf_op jit(solution)/shard_map/while/body/dynamic_update_slice | solution.py:110
  89.7 2.8 %dynamic_update_slice.4 = f32[3,256,256]{2,1,0:T(8,128)S(1)} dynamic-update-slice(f32[3,256,256]{2,1,0:T(8,128)S(1)} %get-tuple-element.257, f32[3,128,128]{2,1,0:T(8,128)S(1)} %maximum_add_fusion.2, s32[]{:T(128)} %constant.154.clone.1..sunk, s32[]{:T(128)S(6)} %select_n.138, s32[]{:T(128)S(6)} %select_n.139) | dynamic-update-slice | bytes 393220 | tf_op jit(solution)/shard_map/while/body/dynamic_update_slice | solution.py:110
  100.5 3.0 %dynamic_update_slice.4 = f32[3,256,256]{2,1,0:T(8,128)S(1)} dynamic-update-slice(f32[3,256,256]{2,1,0:T(8,128)S(1)} %get-tuple-element.257, f32[3,128,128]{2,1,0:T(8,128)S(1)} %maximum_add_fusion.2, s32[]{:T(128)} %constant.154.clone.1..sunk, s32[]{:T(128)S(6)} %select_n.138, s32[]{:T(128)S(6)} %select_n.139) | dynamic-update-slice | bytes 393220 | tf_op jit(solution)/shard_map/while/body/dynamic_update_slice | solution.py:110
  111.5 2.9 %dynamic_update_slice.4 = f32[3,256,256]{2,1,0:T(8,128)S(1)} dynamic-update-slice(f32[3,256,256]{2,1,0:T(8,128)S(1)} %get-tuple-element.257, f32[3,128,128]{2,1,0:T(8,128)S(1)} %maximum_add_fusion.2, s32[]{:T(128)} %constant.154.clone.1..sunk, s32[]{:T(128)S(6)} %select_n.138, s32[]{:T(128)S(6)} %select_n.139) | dynamic-update-slice | bytes 393220 | tf_op jit(solution)/shard_map/while/body/dynamic_update_slice | solution.py:110
  115.1 1.3 collective-permute-start
  116.4 1.0 collective-permute-done
  117.5 1.3 collective-permute-start.1
  118.8 2.0 collective-permute-done.1
  121.0 1.3 collective-permute-start.2
  122.3 1.3 collective-permute-start.3
  123.6 1.8 collective-permute-done.2
  125.6 1.3 scatter-add.16
  126.9 57.1 %collective-permute-done.3 = f32[3,128,64]{2,1,0:T(8,128)S(1)} collective-permute-done((f32[3,128,64]{2,1,0:T(8,128)S(1)}, f32[3,128,64]{2,1,0:T(8,128)S(1)}, u32[]{:S(2)}, u32[]{:S(2)}) %collective-permute-start.3) | collective-permute-done | bytes 98336 | tf_op jit(solution)/shard_map/ppermute | solution.py:23
  184.6 0.8 fusion.145
  185.4 4.8 %collective-permute-start.4 = (bf16[2,64,128]{2,1,0:T(8,128)(2,1)S(1)}, bf16[2,64,128]{2,1,0:T(8,128)(2,1)S(1)}, u32[]{:S(2)}, u32[]{:S(2)}) collective-permute-start(bf16[2,64,128]{2,1,0:T(8,128)(2,1)S(1)} %get-tuple-element.161), channel_id=1, source_target_pairs={{0,8},{8,16},{16,24},{1,9},{9,17},{17,25},{2,10},{10,18},{18,26},{... | collective-permute-start | bytes 98312 | tf_op jit(solution)/shard_map/ppermute | solution.py:34
  190.2 1.3 collective-permute-start.5
  191.5 2.3 collective-permute-done.5
  193.9 1.5 tile.4
  195.4 4.2 %all-to-all-start.2 = ((bf16[2,256,1024]{1,0,2:T(2,128)(2,1)}), bf16[2,256,1024]{1,0,2:T(2,128)(2,1)S(1)}, u32[]{:S(2)}, u32[]{:S(2)}) async-start(bf16[2,256,1024]{1,0,2:T(2,128)(2,1)} %bitcast.15), calls=%async_computation.2 | async-start | bytes 2097152 | tf_op jit(solution)/shard_map/all_to_all | solution.py:15
  199.7 26.4 %all-to-all-done.2 = bf16[2,256,1024]{1,0,2:T(2,128)(2,1)S(1)} async-done(((bf16[2,256,1024]{1,0,2:T(2,128)(2,1)}), bf16[2,256,1024]{1,0,2:T(2,128)(2,1)S(1)}, u32[]{:S(2)}, u32[]{:S(2)}) %all-to-all-start.2) | async-done | bytes 1048608 | tf_op jit(solution)/shard_map/all_to_all | solution.py:15
  226.1 1.5 pad.13
  227.7 9.1 %while.16 = (s32[]{:T(128)}, bf16[2,256,1152]{1,0,2:T(2,128)(2,1)S(1)}, s32[4,3]{1,0:T(4,128)S(1)}, bf16[4,2,128,128]{3,2,0,1:T(8,128)(2,1)S(1)}, s32[]{:T(128)}) while((s32[]{:T(128)}, bf16[2,256,1152]{1,0,2:T(2,128)(2,1)S(1)}, s32[4,3]{1,0:T(4,128)S(1)}, bf16[4,2,128,128]{3,2,0,1:T(8,128)(2,1)S(1)}, s32[]{:T(128)}) %tuple.76), condition=%wide.while_cond.4, body=%wide.while_body.4.sunk | while | flops 2 | bytes 393333 | solution.py:88
  228.3 1.4 constant_dynamic-slice_fusion.9
  230.6 1.4 constant_dynamic-slice_fusion.9
  232.8 1.4 constant_dynamic-slice_fusion.9
  235.1 1.4 constant_dynamic-slice_fusion.9
  236.9 0.8 fusion.18
  237.7 0.8 fusion.17
  238.4 0.8 fusion.7
  239.2 0.7 fusion.28
  239.9 0.7 fusion.42
  240.7 0.7 fusion.6
  241.4 0.7 convolution_add_fusion.2
  242.2 0.7 convolution_subtract_fusion.2
  242.9 0.8 fusion.34
  243.7 0.8 fusion.38
  244.5 0.8 fusion.5
  245.3 0.7 fusion.36
  246.0 0.7 fusion.23
  246.8 0.8 fusion.4
  247.6 0.7 fusion.11
  248.3 0.7 fusion.10
  249.1 0.7 copy.103
  (69 shorter events, 11.8 us)
Async XLA Ops:
  4.9 13.8 %all-to-all-start = ((s32[8,2,3]{2,1,0:T(2,128)}), s32[8,2,3]{2,1,0:T(2,128)S(1)}, u32[]{:S(2)}, u32[]{:S(2)}) async-start(s32[8,2,3]{2,1,0:T(2,128)} %bitcast.10), calls=%async_computation | async-start | bytes 16384 | tf_op jit(solution)/shard_map/all_to_all | solution.py:162
  17.7 6.1 %copy-start.1 = (f32[2,128,128]{2,1,0:T(8,128)S(1)}, f32[2,128,128]{2,1,0:T(8,128)}, u32[]{:S(2)}) copy-start(f32[2,128,128]{2,1,0:T(8,128)} %param.17) | copy-start | bytes 393220
  18.7 30.5 %all-to-all-start.1 = ((bf16[16,2,128,128]{3,2,1,0:T(8,128)(2,1)}), bf16[16,2,128,128]{3,2,1,0:T(8,128)(2,1)S(1)}, u32[]{:S(2)}, u32[]{:S(2)}) async-start(bf16[16,2,128,128]{3,2,1,0:T(8,128)(2,1)} %scatter_fusion), calls=%async_computation.1 | async-start | bytes 2097152 | tf_op jit(solution)/shard_map/all_to_all | solution.py:161
  115.1 2.4 collective-permute-start
  117.5 3.3 %collective-permute-start.1 = (f32[3,64,256]{2,1,0:T(8,128)S(1)}, f32[3,64,256]{2,1,0:T(8,128)S(1)}, u32[]{:S(2)}, u32[]{:S(2)}) collective-permute-start(f32[3,64,256]{2,1,0:T(8,128)S(1)} %get-tuple-element.153), channel_id=1, source_target_pairs={{8,0},{16,8},{24,16},{9,1},{17,9},{25,17},{10,2},{18,10},{26,18},{... | collective-permute-start | bytes 589832 | tf_op jit(solution)/shard_map/ppermute | solution.py:23
  121.0 4.5 %collective-permute-start.2 = (f32[3,128,64]{2,1,0:T(8,128)S(1)}, f32[3,128,64]{2,1,0:T(8,128)S(1)}, u32[]{:S(2)}, u32[]{:S(2)}) collective-permute-start(f32[3,128,64]{2,1,0:T(8,128)S(1)} %get-tuple-element.152), channel_id=1, source_target_pairs={{0,1},{1,2},{2,3},{3,4},{4,5},{5,6},{6,7},{8,9},{9,10},{10,11},{11... | collective-permute-start | bytes 294920 | tf_op jit(solution)/shard_map/ppermute | solution.py:23
  122.3 61.7 %collective-permute-start.3 = (f32[3,128,64]{2,1,0:T(8,128)S(1)}, f32[3,128,64]{2,1,0:T(8,128)S(1)}, u32[]{:S(2)}, u32[]{:S(2)}) collective-permute-start(f32[3,128,64]{2,1,0:T(8,128)S(1)} %get-tuple-element.151), channel_id=1, source_target_pairs={{1,0},{2,1},{3,2},{4,3},{5,4},{6,5},{7,6},{9,8},{10,9},{11,10},{12... | collective-permute-start | bytes 294920 | tf_op jit(solution)/shard_map/ppermute | solution.py:23
  185.4 6.1 %collective-permute-start.4 = (bf16[2,64,128]{2,1,0:T(8,128)(2,1)S(1)}, bf16[2,64,128]{2,1,0:T(8,128)(2,1)S(1)}, u32[]{:S(2)}, u32[]{:S(2)}) collective-permute-start(bf16[2,64,128]{2,1,0:T(8,128)(2,1)S(1)} %get-tuple-element.161), channel_id=1, source_target_pairs={{0,8},{8,16},{16,24},{1,9},{9,17},{17,25},{2,10},{10,18},{18,26},{... | collective-permute-start | bytes 98312 | tf_op jit(solution)/shard_map/ppermute | solution.py:34
  190.2 3.6 %collective-permute-start.5 = (bf16[2,64,128]{2,1,0:T(8,128)(2,1)S(1)}, bf16[2,64,128]{2,1,0:T(8,128)(2,1)S(1)}, u32[]{:S(2)}, u32[]{:S(2)}) collective-permute-start(bf16[2,64,128]{2,1,0:T(8,128)(2,1)S(1)} %get-tuple-element.162), channel_id=1, source_target_pairs={{8,0},{16,8},{24,16},{9,1},{17,9},{25,17},{10,2},{18,10},{26,18},{... | collective-permute-start | bytes 98312 | tf_op jit(solution)/shard_map/ppermute | solution.py:36
  195.4 30.7 %all-to-all-start.2 = ((bf16[2,256,1024]{1,0,2:T(2,128)(2,1)}), bf16[2,256,1024]{1,0,2:T(2,128)(2,1)S(1)}, u32[]{:S(2)}, u32[]{:S(2)}) async-start(bf16[2,256,1024]{1,0,2:T(2,128)(2,1)} %bitcast.15), calls=%async_computation.2 | async-start | bytes 2097152 | tf_op jit(solution)/shard_map/all_to_all | solution.py:15
  240.7 2.2 copy-start
